TPU v7x, 128 devices: a whole 4x4x4 slice. The times are simulated.
128 devices in a mesh: fsdp: 32 (over x, y, core), tensor: 4 (over z).
Axes of the slice: x: 4, y: 4, z: 4, core: 2. Of those that a mesh axis runs over, the one named last changes fastest.
Arguments:
- tokens: bfloat16 [4096, 4096], P(('fsdp', 'tensor')), may hold values from -6 to 6
- gate_blocks: bfloat16 [4, 544, 128, 128], P('tensor', 'fsdp'), may hold values from -0.125 to 0.125
- gate_index: int32 [4, 544], P('tensor', 'fsdp'), may hold values from 0 to 896, as said below
- up_blocks: bfloat16 [4, 544, 128, 128], P('tensor', 'fsdp'), may hold values from -0.125 to 0.125
- up_index: int32 [4, 544], P('tensor', 'fsdp'), may hold values from 0 to 896, as said below
- d_hidden: bfloat16 [4096, 14336], P('fsdp', 'tensor'), may hold values from -6 to 6
Outputs:
- hidden: bfloat16 [4096, 14336], P('fsdp', 'tensor')
- d_tokens: bfloat16 [4096, 4096], P(('fsdp', 'tensor'))
Inputs may be any that keep to these rules, and one draw needn't show every extreme that they name: `gate_index`: row t, slots f * 17 to (f + 1) * 17 - 1 belong to fsdp index f: its live slots come first and hold distinct values r * 28 + c with r among row blocks f * 1 to (f + 1) - 1; the remaining slots hold 896. Each such shard has 11 to 17 live slots, both reached in every row; shards 2i and 2i + 1 together hold exactly 28 live slots. `up_index`: as for gate_index, drawn independently.
All inputs are finite; a program needn't handle non-finite values.
Results may differ from a plain program's by a relative error of at most 0.005.
Values may be sent and summed in bfloat16 or wider, within the bound.
No kernel may reach another device: no remote copies, remote signals or barrier semaphores. Data moves between devices by JAX's collectives and lax.ppermute only.
A program may use at most 128 MiB of HBM per device.

v0:
```python
import jax
import jax.numpy as jnp
from jax import lax
from jax.sharding import PartitionSpec as P


def positions(block_index, row_blocks, col_blocks):
    valid = block_index < row_blocks * col_blocks
    row_of = jnp.minimum(block_index // col_blocks, row_blocks - 1)
    col_of = block_index % col_blocks
    row_target = jnp.where(valid, row_of, row_blocks)
    col_target = jnp.where(valid, col_of, col_blocks)
    return (row_of, col_of, row_target, col_target)


def forward_group(total, rows_split, blocks, block_index, row_blocks, col_blocks):
    row_of, col_of, row_target, col_target = positions(block_index, row_blocks, col_blocks)
    picked = jnp.take(rows_split, row_of, axis=1)
    product = jnp.einsum("tsk,skn->tsn", picked, blocks, preferred_element_type=jnp.float32)
    return total.at[:, col_target].add(product, mode="drop")


def backward_group(total, grad_split, blocks, block_index, row_blocks, col_blocks):
    row_of, col_of, row_target, col_target = positions(block_index, row_blocks, col_blocks)
    chosen = jnp.take(grad_split, col_of, axis=1)
    product = jnp.einsum("tsn,skn->tsk", chosen, blocks, preferred_element_type=jnp.float32)
    return total.at[:, row_target].add(product, mode="drop")


def shards(tokens, gate_blocks, gate_index, up_blocks, up_index, d_hidden):
    block = gate_blocks.shape[-1]
    gathered_rows = lax.all_gather(tokens, "tensor", axis=0, tiled=True)
    row_count = gathered_rows.shape[0]
    model_width = gathered_rows.shape[1]
    row_blocks = model_width // block
    local_units = d_hidden.shape[1]
    col_blocks = local_units // block
    shard_count = lax.axis_size("fsdp")
    own_gate, own_gate_index = (gate_blocks[0], gate_index[0])
    own_up, own_up_index = (up_blocks[0], up_index[0])
    all_gate, all_gate_index, all_up, all_up_index = (
        lax.all_gather(own_gate, "fsdp", axis=0, tiled=True),
        lax.all_gather(own_gate_index, "fsdp", axis=0, tiled=True),
        lax.all_gather(own_up, "fsdp", axis=0, tiled=True),
        lax.all_gather(own_up_index, "fsdp", axis=0, tiled=True),
    )
    per_shard = own_gate.shape[0]
    group_shards = 4
    group_count = shard_count // group_shards
    group_slots = group_shards * per_shard
    grouped = (
        all_gate.reshape(group_count, group_slots, block, block),
        all_gate_index.reshape(group_count, group_slots),
        all_up.reshape(group_count, group_slots, block, block),
        all_up_index.reshape(group_count, group_slots),
    )
    rows_split = gathered_rows.reshape(row_count, row_blocks, block)

    def forward_step(carry, pieces):
        gate_acc, up_acc = carry
        gate_acc = forward_group(gate_acc, rows_split, pieces[0], pieces[1], row_blocks, col_blocks)
        up_acc = forward_group(up_acc, rows_split, pieces[2], pieces[3], row_blocks, col_blocks)
        return ((gate_acc, up_acc), None)

    empty_cols = jnp.zeros((row_count, col_blocks, block), jnp.float32)
    (gate, up), _ = lax.scan(forward_step, (empty_cols, empty_cols), grouped)
    gate = gate.reshape(row_count, local_units)
    up = up.reshape(row_count, local_units)
    sig = jax.nn.sigmoid(gate)
    active = gate * sig
    hidden = (active * up).astype(jnp.bfloat16)
    d_slice = d_hidden.astype(jnp.float32)
    d_gate = (
        (d_slice * up * sig * (1.0 + gate * (1.0 - sig)))
        .astype(jnp.bfloat16)
        .reshape(row_count, col_blocks, block)
    )
    d_up = (d_slice * active).astype(jnp.bfloat16).reshape(row_count, col_blocks, block)

    def backward_step(total, pieces):
        total = backward_group(total, d_gate, pieces[0], pieces[1], row_blocks, col_blocks)
        total = backward_group(total, d_up, pieces[2], pieces[3], row_blocks, col_blocks)
        return (total, None)

    empty_rows = jnp.zeros((row_count, row_blocks, block), jnp.float32)
    partial_grad, _ = lax.scan(backward_step, empty_rows, grouped)
    partial_grad = partial_grad.reshape(row_count, model_width)
    d_tokens = lax.psum_scatter(partial_grad, "tensor", scatter_dimension=0, tiled=True).astype(
        jnp.bfloat16
    )
    return (hidden, d_tokens)


def solution(mesh):
    in_specs = (
        P(("fsdp", "tensor"), None),
        P("tensor", "fsdp", None, None),
        P("tensor", "fsdp"),
        P("tensor", "fsdp", None, None),
        P("tensor", "fsdp"),
        P("fsdp", "tensor"),
    )
    out_specs = (P("fsdp", "tensor"), P(("fsdp", "tensor"), None))
    return jax.shard_map(shards, mesh=mesh, in_specs=in_specs, out_specs=out_specs, check_vma=False)
```

profile of v0, /device:TPU:1, one launch (start us, length us, event | category | flops | bytes accessed | tf_op | source)
XLA Modules:
  0.0 901.3 jit_solution(12688166231259519169)
XLA Ops:
  12.8 14.7 %all-reduce.2 = (s32[544]{0:T(1024)S(1)}, s32[544]{0:T(1024)S(1)}) all-reduce(s32[544]{0:T(1024)S(1)} %bitcast_dynamic-update-slice_fusion.1, s32[544]{0:T(1024)S(1)} %bitcast_dynamic-update-slice_fusion), channel_id=2, replica_groups=mesh['fsdp'=32,'tensor'=4] {'fsdp'}, use_global_device_ids=true, to_apply=%add | all-reduce | flops 1088 | bytes 8704
  38.5 76.5 %all-gather.10.cloned.1.call-done = bf16[1,544,128,128]{3,2,0,1:T(8,128)(2,1)} async-done(((bf16[1,17,128,128]{3,2,0,1:T(8,128)(2,1)}), bf16[1,544,128,128]{3,2,0,1:T(8,128)(2,1)}) %all-gather.10.cloned.1.call-update) | async-done | bytes 17825808 | tf_op jit(solution)/shard_map/all_gather | solution.py:42
  115.0 76.6 %all-gather.12.cloned.1.call-done = bf16[1,544,128,128]{3,2,0,1:T(8,128)(2,1)} async-done(((bf16[1,17,128,128]{3,2,0,1:T(8,128)(2,1)}), bf16[1,544,128,128]{3,2,0,1:T(8,128)(2,1)}) %all-gather.12.cloned.1.call-update) | async-done | bytes 17825808 | tf_op jit(solution)/shard_map/all_gather | solution.py:44
  193.3 340.1 %while.28 = (s32[]{:T(128)}, f32[128,28,128]{2,0,1:T(8,128)S(1)}, f32[128,28,128]{2,0,1:T(8,128)}, s32[8,68]{1,0:T(8,128)S(1)}, bf16[8,68,128,128]{3,2,1,0:T(8,1...) while((s32[]{:T(128)}, f32[128,28,128]{2,0,1:T(8,128)S(1)}, ...), condition=%wide.region_3.5_spmd, body=%wide.region_0.4_spmd.sunk | while | flops 574887424 | bytes 53490772 | solution.py:66
  201.0 17.0 %scatter_fusion.1 = f32[128,28,128]{2,0,1:T(8,128)} fusion(f32[128,28,128]{2,0,1:T(8,128)} %get-tuple-element.504, s32[68]{0:T(128)S(1)} %get-tuple-element.476, f32[68,128,128]{2,1,0:T(8,128)} %fusion.70), kind=kCustom, calls=%fused_computation.5.clone.1 | custom fusion | flops 1114112 | bytes 13369616 | tf_op jit(solution)/shard_map/while/body/eval_jaxpr/scatter-add | solution.py:20
  225.6 10.6 %scatter_fusion = f32[128,28,128]{2,0,1:T(8,128)S(1)} fusion(f32[128,28,128]{2,0,1:T(8,128)S(1)} %get-tuple-element.503, s32[68]{0:T(128)S(1)} %get-tuple-element.473, f32[68,128,128]{2,1,0:T(8,128)} %fusion.69), kind=kCustom, calls=%fused_computation.4.clone.1 | custom fusion | flops 1114112 | bytes 13369616 | tf_op jit(solution)/shard_map/while/body/eval_jaxpr/scatter-add | solution.py:20
  243.8 16.4 %scatter_fusion.1 = f32[128,28,128]{2,0,1:T(8,128)} fusion(f32[128,28,128]{2,0,1:T(8,128)} %get-tuple-element.504, s32[68]{0:T(128)S(1)} %get-tuple-element.476, f32[68,128,128]{2,1,0:T(8,128)} %fusion.70), kind=kCustom, calls=%fused_computation.5.clone.1 | custom fusion | flops 1114112 | bytes 13369616 | tf_op jit(solution)/shard_map/while/body/eval_jaxpr/scatter-add | solution.py:20
  267.9 10.6 %scatter_fusion = f32[128,28,128]{2,0,1:T(8,128)S(1)} fusion(f32[128,28,128]{2,0,1:T(8,128)S(1)} %get-tuple-element.503, s32[68]{0:T(128)S(1)} %get-tuple-element.473, f32[68,128,128]{2,1,0:T(8,128)} %fusion.69), kind=kCustom, calls=%fused_computation.4.clone.1 | custom fusion | flops 1114112 | bytes 13369616 | tf_op jit(solution)/shard_map/while/body/eval_jaxpr/scatter-add | solution.py:20
  286.2 16.9 %scatter_fusion.1 = f32[128,28,128]{2,0,1:T(8,128)} fusion(f32[128,28,128]{2,0,1:T(8,128)} %get-tuple-element.504, s32[68]{0:T(128)S(1)} %get-tuple-element.476, f32[68,128,128]{2,1,0:T(8,128)} %fusion.70), kind=kCustom, calls=%fused_computation.5.clone.1 | custom fusion | flops 1114112 | bytes 13369616 | tf_op jit(solution)/shard_map/while/body/eval_jaxpr/scatter-add | solution.py:20
  310.7 10.6 %scatter_fusion = f32[128,28,128]{2,0,1:T(8,128)S(1)} fusion(f32[128,28,128]{2,0,1:T(8,128)S(1)} %get-tuple-element.503, s32[68]{0:T(128)S(1)} %get-tuple-element.473, f32[68,128,128]{2,1,0:T(8,128)} %fusion.69), kind=kCustom, calls=%fused_computation.4.clone.1 | custom fusion | flops 1114112 | bytes 13369616 | tf_op jit(solution)/shard_map/while/body/eval_jaxpr/scatter-add | solution.py:20
  329.0 16.4 %scatter_fusion.1 = f32[128,28,128]{2,0,1:T(8,128)} fusion(f32[128,28,128]{2,0,1:T(8,128)} %get-tuple-element.504, s32[68]{0:T(128)S(1)} %get-tuple-element.476, f32[68,128,128]{2,1,0:T(8,128)} %fusion.70), kind=kCustom, calls=%fused_computation.5.clone.1 | custom fusion | flops 1114112 | bytes 13369616 | tf_op jit(solution)/shard_map/while/body/eval_jaxpr/scatter-add | solution.py:20
  353.0 10.6 %scatter_fusion = f32[128,28,128]{2,0,1:T(8,128)S(1)} fusion(f32[128,28,128]{2,0,1:T(8,128)S(1)} %get-tuple-element.503, s32[68]{0:T(128)S(1)} %get-tuple-element.473, f32[68,128,128]{2,1,0:T(8,128)} %fusion.69), kind=kCustom, calls=%fused_computation.4.clone.1 | custom fusion | flops 1114112 | bytes 13369616 | tf_op jit(solution)/shard_map/while/body/eval_jaxpr/scatter-add | solution.py:20
  371.3 16.6 %scatter_fusion.1 = f32[128,28,128]{2,0,1:T(8,128)} fusion(f32[128,28,128]{2,0,1:T(8,128)} %get-tuple-element.504, s32[68]{0:T(128)S(1)} %get-tuple-element.476, f32[68,128,128]{2,1,0:T(8,128)} %fusion.70), kind=kCustom, calls=%fused_computation.5.clone.1 | custom fusion | flops 1114112 | bytes 13369616 | tf_op jit(solution)/shard_map/while/body/eval_jaxpr/scatter-add | solution.py:20
  395.5 10.6 %scatter_fusion = f32[128,28,128]{2,0,1:T(8,128)S(1)} fusion(f32[128,28,128]{2,0,1:T(8,128)S(1)} %get-tuple-element.503, s32[68]{0:T(128)S(1)} %get-tuple-element.473, f32[68,128,128]{2,1,0:T(8,128)} %fusion.69), kind=kCustom, calls=%fused_computation.4.clone.1 | custom fusion | flops 1114112 | bytes 13369616 | tf_op jit(solution)/shard_map/while/body/eval_jaxpr/scatter-add | solution.py:20
  413.8 16.4 %scatter_fusion.1 = f32[128,28,128]{2,0,1:T(8,128)} fusion(f32[128,28,128]{2,0,1:T(8,128)} %get-tuple-element.504, s32[68]{0:T(128)S(1)} %get-tuple-element.476, f32[68,128,128]{2,1,0:T(8,128)} %fusion.70), kind=kCustom, calls=%fused_computation.5.clone.1 | custom fusion | flops 1114112 | bytes 13369616 | tf_op jit(solution)/shard_map/while/body/eval_jaxpr/scatter-add | solution.py:20
  437.8 10.6 %scatter_fusion = f32[128,28,128]{2,0,1:T(8,128)S(1)} fusion(f32[128,28,128]{2,0,1:T(8,128)S(1)} %get-tuple-element.503, s32[68]{0:T(128)S(1)} %get-tuple-element.473, f32[68,128,128]{2,1,0:T(8,128)} %fusion.69), kind=kCustom, calls=%fused_computation.4.clone.1 | custom fusion | flops 1114112 | bytes 13369616 | tf_op jit(solution)/shard_map/while/body/eval_jaxpr/scatter-add | solution.py:20
  456.1 16.4 %scatter_fusion.1 = f32[128,28,128]{2,0,1:T(8,128)} fusion(f32[128,28,128]{2,0,1:T(8,128)} %get-tuple-element.504, s32[68]{0:T(128)S(1)} %get-tuple-element.476, f32[68,128,128]{2,1,0:T(8,128)} %fusion.70), kind=kCustom, calls=%fused_computation.5.clone.1 | custom fusion | flops 1114112 | bytes 13369616 | tf_op jit(solution)/shard_map/while/body/eval_jaxpr/scatter-add | solution.py:20
  480.1 10.6 %scatter_fusion = f32[128,28,128]{2,0,1:T(8,128)S(1)} fusion(f32[128,28,128]{2,0,1:T(8,128)S(1)} %get-tuple-element.503, s32[68]{0:T(128)S(1)} %get-tuple-element.473, f32[68,128,128]{2,1,0:T(8,128)} %fusion.69), kind=kCustom, calls=%fused_computation.4.clone.1 | custom fusion | flops 1114112 | bytes 13369616 | tf_op jit(solution)/shard_map/while/body/eval_jaxpr/scatter-add | solution.py:20
  498.4 16.8 %scatter_fusion.1 = f32[128,28,128]{2,0,1:T(8,128)} fusion(f32[128,28,128]{2,0,1:T(8,128)} %get-tuple-element.504, s32[68]{0:T(128)S(1)} %get-tuple-element.476, f32[68,128,128]{2,1,0:T(8,128)} %fusion.70), kind=kCustom, calls=%fused_computation.5.clone.1 | custom fusion | flops 1114112 | bytes 13369616 | tf_op jit(solution)/shard_map/while/body/eval_jaxpr/scatter-add | solution.py:20
  522.9 10.6 %scatter_fusion = f32[128,28,128]{2,0,1:T(8,128)S(1)} fusion(f32[128,28,128]{2,0,1:T(8,128)S(1)} %get-tuple-element.503, s32[68]{0:T(128)S(1)} %get-tuple-element.473, f32[68,128,128]{2,1,0:T(8,128)} %fusion.69), kind=kCustom, calls=%fused_computation.4.clone.1 | custom fusion | flops 1114112 | bytes 13369616 | tf_op jit(solution)/shard_map/while/body/eval_jaxpr/scatter-add | solution.py:20
  545.3 315.6 %while.29 = (s32[]{:T(128)}, f32[128,32,128]{2,0,1:T(8,128)S(1)}, s32[8,68]{1,0:T(8,128)S(1)}, bf16[8,68,128,128]{3,2,1,0:T(8,128)(2,1)}, bf16[128,28,128]{2,0,1...) while((s32[]{:T(128)}, f32[128,32,128]{2,0,1:T(8,128)S(1)}, ...), condition=%wide.region_7.10_spmd, body=%wide.region_4.9_spmd.sunk | while | flops 574887424 | bytes 53490772 | solution.py:86
  554.1 10.6 %scatter_fusion.2 = f32[128,32,128]{2,0,1:T(8,128)S(1)} fusion(f32[128,32,128]{2,0,1:T(8,128)S(1)} %get-tuple-element.530, s32[68]{0:T(128)S(1)} %get-tuple-element.487, f32[68,128,128]{2,1,0:T(8,128)} %fusion.76), kind=kCustom, calls=%fused_computation.6.clone.1 | custom fusion | flops 1114112 | bytes 13369616 | tf_op jit(solution)/shard_map/while/body/eval_jaxpr/scatter-add | solution.py:27
  593.5 10.6 %scatter_fusion.2 = f32[128,32,128]{2,0,1:T(8,128)S(1)} fusion(f32[128,32,128]{2,0,1:T(8,128)S(1)} %get-tuple-element.530, s32[68]{0:T(128)S(1)} %get-tuple-element.487, f32[68,128,128]{2,1,0:T(8,128)} %fusion.76), kind=kCustom, calls=%fused_computation.6.clone.1 | custom fusion | flops 1114112 | bytes 13369616 | tf_op jit(solution)/shard_map/while/body/eval_jaxpr/scatter-add | solution.py:27
  632.9 10.6 %scatter_fusion.2 = f32[128,32,128]{2,0,1:T(8,128)S(1)} fusion(f32[128,32,128]{2,0,1:T(8,128)S(1)} %get-tuple-element.530, s32[68]{0:T(128)S(1)} %get-tuple-element.487, f32[68,128,128]{2,1,0:T(8,128)} %fusion.76), kind=kCustom, calls=%fused_computation.6.clone.1 | custom fusion | flops 1114112 | bytes 13369616 | tf_op jit(solution)/shard_map/while/body/eval_jaxpr/scatter-add | solution.py:27
  672.4 10.6 %scatter_fusion.2 = f32[128,32,128]{2,0,1:T(8,128)S(1)} fusion(f32[128,32,128]{2,0,1:T(8,128)S(1)} %get-tuple-element.530, s32[68]{0:T(128)S(1)} %get-tuple-element.487, f32[68,128,128]{2,1,0:T(8,128)} %fusion.76), kind=kCustom, calls=%fused_computation.6.clone.1 | custom fusion | flops 1114112 | bytes 13369616 | tf_op jit(solution)/shard_map/while/body/eval_jaxpr/scatter-add | solution.py:27
  692.7 10.6 %scatter_fusion.3 = f32[128,32,128]{2,0,1:T(8,128)S(1)} fusion(f32[128,32,128]{2,0,1:T(8,128)S(1)} %scatter_fusion.2, s32[68]{0:T(128)S(1)} %get-tuple-element.490, f32[68,128,128]{2,1,0:T(8,128)} %fusion.77), kind=kCustom, calls=%fused_computation.7.clone.1 | custom fusion | flops 1114112 | bytes 13369616 | tf_op jit(solution)/shard_map/while/body/eval_jaxpr/scatter-add | solution.py:27
  711.8 10.6 %scatter_fusion.2 = f32[128,32,128]{2,0,1:T(8,128)S(1)} fusion(f32[128,32,128]{2,0,1:T(8,128)S(1)} %get-tuple-element.530, s32[68]{0:T(128)S(1)} %get-tuple-element.487, f32[68,128,128]{2,1,0:T(8,128)} %fusion.76), kind=kCustom, calls=%fused_computation.6.clone.1 | custom fusion | flops 1114112 | bytes 13369616 | tf_op jit(solution)/shard_map/while/body/eval_jaxpr/scatter-add | solution.py:27
  751.2 10.6 %scatter_fusion.2 = f32[128,32,128]{2,0,1:T(8,128)S(1)} fusion(f32[128,32,128]{2,0,1:T(8,128)S(1)} %get-tuple-element.530, s32[68]{0:T(128)S(1)} %get-tuple-element.487, f32[68,128,128]{2,1,0:T(8,128)} %fusion.76), kind=kCustom, calls=%fused_computation.6.clone.1 | custom fusion | flops 1114112 | bytes 13369616 | tf_op jit(solution)/shard_map/while/body/eval_jaxpr/scatter-add | solution.py:27
  790.7 10.6 %scatter_fusion.2 = f32[128,32,128]{2,0,1:T(8,128)S(1)} fusion(f32[128,32,128]{2,0,1:T(8,128)S(1)} %get-tuple-element.530, s32[68]{0:T(128)S(1)} %get-tuple-element.487, f32[68,128,128]{2,1,0:T(8,128)} %fusion.76), kind=kCustom, calls=%fused_computation.6.clone.1 | custom fusion | flops 1114112 | bytes 13369616 | tf_op jit(solution)/shard_map/while/body/eval_jaxpr/scatter-add | solution.py:27
  811.0 10.6 %scatter_fusion.3 = f32[128,32,128]{2,0,1:T(8,128)S(1)} fusion(f32[128,32,128]{2,0,1:T(8,128)S(1)} %scatter_fusion.2, s32[68]{0:T(128)S(1)} %get-tuple-element.490, f32[68,128,128]{2,1,0:T(8,128)} %fusion.77), kind=kCustom, calls=%fused_computation.7.clone.1 | custom fusion | flops 1114112 | bytes 13369616 | tf_op jit(solution)/shard_map/while/body/eval_jaxpr/scatter-add | solution.py:27
  830.1 10.6 %scatter_fusion.2 = f32[128,32,128]{2,0,1:T(8,128)S(1)} fusion(f32[128,32,128]{2,0,1:T(8,128)S(1)} %get-tuple-element.530, s32[68]{0:T(128)S(1)} %get-tuple-element.487, f32[68,128,128]{2,1,0:T(8,128)} %fusion.76), kind=kCustom, calls=%fused_computation.6.clone.1 | custom fusion | flops 1114112 | bytes 13369616 | tf_op jit(solution)/shard_map/while/body/eval_jaxpr/scatter-add | solution.py:27
  863.8 29.2 %reduce-scatter.2.cloned.1.call-done = f32[32,4096]{1,0:T(8,128)} async-done(((f32[128,4096]{1,0:T(8,128)}), f32[32,4096]{1,0:T(8,128)}) %reduce-scatter.2.cloned.1.call-update) | async-done | bytes 524304 | tf_op jit(solution)/shard_map/reduce_scatter | solution.py:88
  (172 shorter events, 365.7 us)
Async XLA Ops:
  7.2 29.0 %all-gather.8.cloned.1.call-start = ((), (), s32[]{:S(2)}) async-start(), calls=%async_computation.1 | async-start | bytes 1310720 | tf_op jit(solution)/shard_map/all_gather | solution.py:32
  7.9 107.1 %all-gather.10.cloned.1.call-start = ((), (), s32[]{:S(2)}) async-start(), calls=%async_computation.3 | async-start | bytes 18382848 | tf_op jit(solution)/shard_map/all_gather | solution.py:42
  8.6 183.0 %all-gather.12.cloned.1.call-start = ((), (), s32[]{:S(2)}) async-start(), calls=%async_computation.4 | async-start | bytes 18382848 | tf_op jit(solution)/shard_map/all_gather | solution.py:44
  9.4 883.6 %reduce-scatter.2.cloned.1.call-start = ((), (), s32[]{:S(2)}) async-start(), calls=%async_computation.2 | async-start | bytes 2621440 | tf_op jit(solution)/shard_map/reduce_scatter | solution.py:88
  535.2 2.9 copy-start
  535.2 2.9 copy-start.1
  542.2 1.7 copy-start.3
  860.9 1.6 copy-start.2
Sparse Core Ops, SparseCore 0:
  9.7 26.4 all-gather.7
  38.4 76.5 all-gather.9
  117.3 74.3 all-gather.11
  862.7 30.2 reduce-scatter.1
where the time goes:
time: 908 us; the launch traced here: 901 us
  other arithmetic  393 us (43%)
  waiting for transfers between devices  191 us (21%)
  matrix products  180 us (20%)
  local copies, waits for them, and re-layouts  107 us (12%)
  blocking collectives  14.7 us (2%)
  between operations  14.5 us (2%)
    scatter-add x16, other arithmetic, forward_group(): return total.at[:, col_target].add(product, mode='drop')  218 us
    scatter-add x16, other arithmetic, backward_group(): return total.at[:, row_target].add(product, mode='drop')  169 us
    dot_general x16, matrix products, backward_group(): jnp.einsum('tsn,skn->tsk', chosen, blocks, preferred_element_type=jnp.flo...  97.2 us
    dot_general x16, matrix products, forward_group(): jnp.einsum('tsk,skn->tsn', picked, blocks, preferred_element_type=jnp.flo...  82.6 us
    all_gather x1, waiting for transfers between devices, shards(): lax.all_gather(own_up, 'fsdp', axis=0, tiled=True)  76.6 us
    all_gather x1, waiting for transfers between devices, shards(): lax.all_gather(own_gate, 'fsdp', axis=0, tiled=True)  76.5 us
    gather x16, local copies, waits for them, and re-layouts, backward_group(): chosen = jnp.take(grad_split, col_of, axis=1)  48.5 us
    gather x16, local copies, waits for them, and re-layouts, forward_group(): picked = jnp.take(rows_split, row_of, axis=1)  39 us
  transfers between devices with their start and end apart: 4, of which 4 were waited for; matrix products, arithmetic and copies ran while one was open for 1% of the time, Pallas kernels for 0%

commit v1 on v0

--- a/solution.py
+++ b/solution.py
@@ -41,7 +41,9 @@
     all_gate, all_gate_index, all_up, all_up_index = (
         lax.all_gather(own_gate, "fsdp", axis=0, tiled=True),
         lax.all_gather(own_gate_index, "fsdp", axis=0, tiled=True),
-        lax.all_gather(own_up, "fsdp", axis=0, tiled=True),
+        jnp.concatenate(
+            lax.all_to_all(jnp.stack([own_up] * lax.axis_size("fsdp")), "fsdp", 0, 0), axis=0
+        ),
         lax.all_gather(own_up_index, "fsdp", axis=0, tiled=True),
     )
     per_shard = own_gate.shape[0]

time: 908 us -> 1050 us (1.16)
  blocking collectives: 14.7 us -> 263 us
  waiting for transfers between devices: 191 us -> 77.5 us
    unnamed x1, blocking collectives: 14.7 us -> 263 us
    all_gather x1 -> x0, waiting for transfers between devices: 76.6 us -> none  [shards(): lax.all_gather(own_up, 'fsdp', axis=0, tiled=True)]
    all_gather x1, waiting for transfers between devices: 76.5 us -> 0.01 us  [shards(): lax.all_gather(own_gate, 'fsdp', axis=0, tiled=True)]
    reduce_scatter x1, waiting for transfers between devices: 29.2 us -> 68.6 us  [shards(): lax.psum_scatter(partial_grad, 'tensor', scatter_dimension=0, tiled=True)]
  transfers between devices with their start and end apart: 4 -> 4, of which waited for: 4 -> 2; matrix products, arithmetic and copies ran while one was open for 1% -> 1% of each run, Pallas kernels for 0% -> 0%
where the time goes in v1:
time: 1050 us
  other arithmetic  390 us (37%)
  blocking collectives  263 us (25%)
  matrix products  179 us (17%)
  local copies, waits for them, and re-layouts  112 us (11%)
  waiting for transfers between devices  77.5 us (7%)
  between operations  14.5 us (1%)
    unnamed x1, blocking collectives  263 us
    scatter-add x16, other arithmetic, forward_group(): return total.at[:, col_target].add(product, mode='drop')  214 us
    scatter-add x16, other arithmetic, backward_group(): return total.at[:, row_target].add(product, mode='drop')  169 us
    dot_general x16, matrix products, backward_group(): jnp.einsum('tsn,skn->tsk', chosen, blocks, preferred_element_type=jnp.flo...  97 us
    dot_general x16, matrix products, forward_group(): jnp.einsum('tsk,skn->tsn', picked, blocks, preferred_element_type=jnp.flo...  82.4 us
    reduce_scatter x1, waiting for transfers between devices, shards(): lax.psum_scatter(partial_grad, 'tensor', scatter_dimension=0, tiled=True)  68.6 us
    gather x16, local copies, waits for them, and re-layouts, backward_group(): chosen = jnp.take(grad_split, col_of, axis=1)  48.4 us
    gather x16, local copies, waits for them, and re-layouts, forward_group(): picked = jnp.take(rows_split, row_of, axis=1)  39 us
  transfers between devices with their start and end apart: 4, of which 2 were waited for; matrix products, arithmetic and copies ran while one was open for 1% of the time, Pallas kernels for 0%

profile of v1, /device:TPU:1, one launch (start us, length us, event | category | flops | bytes accessed | tf_op | source)
XLA Modules:
  0.0 1046.2 jit_solution(4213315728137728349)
XLA Ops:
  26.3 263.2 %all-reduce.2 = (s32[544]{0:T(1024)S(1)}, s32[544]{0:T(1024)S(1)}) all-reduce(s32[544]{0:T(1024)S(1)} %bitcast_dynamic-update-slice_fusion.1, s32[544]{0:T(1024)S(1)} %bitcast_dynamic-update-slice_fusion), channel_id=2, replica_groups=mesh['fsdp'=32,'tensor'=4] {'fsdp'}, use_global_device_ids=true, to_apply=%add | all-reduce | flops 1088 | bytes 8704
  302.5 336.7 %while.28 = (s32[]{:T(128)}, f32[128,28,128]{2,0,1:T(8,128)S(1)}, f32[128,28,128]{2,0,1:T(8,128)}, s32[8,68]{1,0:T(8,128)S(1)}, bf16[8,68,128,128]{3,2,1,0:T(8,1...) while((s32[]{:T(128)}, f32[128,28,128]{2,0,1:T(8,128)S(1)}, ...), condition=%wide.region_3.5_spmd, body=%wide.region_0.4_spmd.sunk | while | flops 574887424 | bytes 53490772 | solution.py:68
  310.1 16.5 %scatter_fusion.1 = f32[128,28,128]{2,0,1:T(8,128)} fusion(f32[128,28,128]{2,0,1:T(8,128)} %get-tuple-element.504, s32[68]{0:T(128)S(1)} %get-tuple-element.476, f32[68,128,128]{2,1,0:T(8,128)} %fusion.70), kind=kCustom, calls=%fused_computation.5.clone.1 | custom fusion | flops 1114112 | bytes 13369616 | tf_op jit(solution)/shard_map/while/body/eval_jaxpr/scatter-add | solution.py:20
  334.3 10.6 %scatter_fusion = f32[128,28,128]{2,0,1:T(8,128)S(1)} fusion(f32[128,28,128]{2,0,1:T(8,128)S(1)} %get-tuple-element.503, s32[68]{0:T(128)S(1)} %get-tuple-element.473, f32[68,128,128]{2,1,0:T(8,128)} %fusion.69), kind=kCustom, calls=%fused_computation.4.clone.1 | custom fusion | flops 1114112 | bytes 13369616 | tf_op jit(solution)/shard_map/while/body/eval_jaxpr/scatter-add | solution.py:20
  352.5 16.1 %scatter_fusion.1 = f32[128,28,128]{2,0,1:T(8,128)} fusion(f32[128,28,128]{2,0,1:T(8,128)} %get-tuple-element.504, s32[68]{0:T(128)S(1)} %get-tuple-element.476, f32[68,128,128]{2,1,0:T(8,128)} %fusion.70), kind=kCustom, calls=%fused_computation.5.clone.1 | custom fusion | flops 1114112 | bytes 13369616 | tf_op jit(solution)/shard_map/while/body/eval_jaxpr/scatter-add | solution.py:20
  376.2 10.6 %scatter_fusion = f32[128,28,128]{2,0,1:T(8,128)S(1)} fusion(f32[128,28,128]{2,0,1:T(8,128)S(1)} %get-tuple-element.503, s32[68]{0:T(128)S(1)} %get-tuple-element.473, f32[68,128,128]{2,1,0:T(8,128)} %fusion.69), kind=kCustom, calls=%fused_computation.4.clone.1 | custom fusion | flops 1114112 | bytes 13369616 | tf_op jit(solution)/shard_map/while/body/eval_jaxpr/scatter-add | solution.py:20
  394.5 16.5 %scatter_fusion.1 = f32[128,28,128]{2,0,1:T(8,128)} fusion(f32[128,28,128]{2,0,1:T(8,128)} %get-tuple-element.504, s32[68]{0:T(128)S(1)} %get-tuple-element.476, f32[68,128,128]{2,1,0:T(8,128)} %fusion.70), kind=kCustom, calls=%fused_computation.5.clone.1 | custom fusion | flops 1114112 | bytes 13369616 | tf_op jit(solution)/shard_map/while/body/eval_jaxpr/scatter-add | solution.py:20
  418.6 10.6 %scatter_fusion = f32[128,28,128]{2,0,1:T(8,128)S(1)} fusion(f32[128,28,128]{2,0,1:T(8,128)S(1)} %get-tuple-element.503, s32[68]{0:T(128)S(1)} %get-tuple-element.473, f32[68,128,128]{2,1,0:T(8,128)} %fusion.69), kind=kCustom, calls=%fused_computation.4.clone.1 | custom fusion | flops 1114112 | bytes 13369616 | tf_op jit(solution)/shard_map/while/body/eval_jaxpr/scatter-add | solution.py:20
  436.8 16.1 %scatter_fusion.1 = f32[128,28,128]{2,0,1:T(8,128)} fusion(f32[128,28,128]{2,0,1:T(8,128)} %get-tuple-element.504, s32[68]{0:T(128)S(1)} %get-tuple-element.476, f32[68,128,128]{2,1,0:T(8,128)} %fusion.70), kind=kCustom, calls=%fused_computation.5.clone.1 | custom fusion | flops 1114112 | bytes 13369616 | tf_op jit(solution)/shard_map/while/body/eval_jaxpr/scatter-add | solution.py:20
  460.5 10.6 %scatter_fusion = f32[128,28,128]{2,0,1:T(8,128)S(1)} fusion(f32[128,28,128]{2,0,1:T(8,128)S(1)} %get-tuple-element.503, s32[68]{0:T(128)S(1)} %get-tuple-element.473, f32[68,128,128]{2,1,0:T(8,128)} %fusion.69), kind=kCustom, calls=%fused_computation.4.clone.1 | custom fusion | flops 1114112 | bytes 13369616 | tf_op jit(solution)/shard_map/while/body/eval_jaxpr/scatter-add | solution.py:20
  478.8 16.1 %scatter_fusion.1 = f32[128,28,128]{2,0,1:T(8,128)} fusion(f32[128,28,128]{2,0,1:T(8,128)} %get-tuple-element.504, s32[68]{0:T(128)S(1)} %get-tuple-element.476, f32[68,128,128]{2,1,0:T(8,128)} %fusion.70), kind=kCustom, calls=%fused_computation.5.clone.1 | custom fusion | flops 1114112 | bytes 13369616 | tf_op jit(solution)/shard_map/while/body/eval_jaxpr/scatter-add | solution.py:20
  502.4 10.6 %scatter_fusion = f32[128,28,128]{2,0,1:T(8,128)S(1)} fusion(f32[128,28,128]{2,0,1:T(8,128)S(1)} %get-tuple-element.503, s32[68]{0:T(128)S(1)} %get-tuple-element.473, f32[68,128,128]{2,1,0:T(8,128)} %fusion.69), kind=kCustom, calls=%fused_computation.4.clone.1 | custom fusion | flops 1114112 | bytes 13369616 | tf_op jit(solution)/shard_map/while/body/eval_jaxpr/scatter-add | solution.py:20
  520.7 16.0 %scatter_fusion.1 = f32[128,28,128]{2,0,1:T(8,128)} fusion(f32[128,28,128]{2,0,1:T(8,128)} %get-tuple-element.504, s32[68]{0:T(128)S(1)} %get-tuple-element.476, f32[68,128,128]{2,1,0:T(8,128)} %fusion.70), kind=kCustom, calls=%fused_computation.5.clone.1 | custom fusion | flops 1114112 | bytes 13369616 | tf_op jit(solution)/shard_map/while/body/eval_jaxpr/scatter-add | solution.py:20
  544.3 10.6 %scatter_fusion = f32[128,28,128]{2,0,1:T(8,128)S(1)} fusion(f32[128,28,128]{2,0,1:T(8,128)S(1)} %get-tuple-element.503, s32[68]{0:T(128)S(1)} %get-tuple-element.473, f32[68,128,128]{2,1,0:T(8,128)} %fusion.69), kind=kCustom, calls=%fused_computation.4.clone.1 | custom fusion | flops 1114112 | bytes 13369616 | tf_op jit(solution)/shard_map/while/body/eval_jaxpr/scatter-add | solution.py:20
  562.6 16.1 %scatter_fusion.1 = f32[128,28,128]{2,0,1:T(8,128)} fusion(f32[128,28,128]{2,0,1:T(8,128)} %get-tuple-element.504, s32[68]{0:T(128)S(1)} %get-tuple-element.476, f32[68,128,128]{2,1,0:T(8,128)} %fusion.70), kind=kCustom, calls=%fused_computation.5.clone.1 | custom fusion | flops 1114112 | bytes 13369616 | tf_op jit(solution)/shard_map/while/body/eval_jaxpr/scatter-add | solution.py:20
  586.3 10.6 %scatter_fusion = f32[128,28,128]{2,0,1:T(8,128)S(1)} fusion(f32[128,28,128]{2,0,1:T(8,128)S(1)} %get-tuple-element.503, s32[68]{0:T(128)S(1)} %get-tuple-element.473, f32[68,128,128]{2,1,0:T(8,128)} %fusion.69), kind=kCustom, calls=%fused_computation.4.clone.1 | custom fusion | flops 1114112 | bytes 13369616 | tf_op jit(solution)/shard_map/while/body/eval_jaxpr/scatter-add | solution.py:20
  604.6 16.4 %scatter_fusion.1 = f32[128,28,128]{2,0,1:T(8,128)} fusion(f32[128,28,128]{2,0,1:T(8,128)} %get-tuple-element.504, s32[68]{0:T(128)S(1)} %get-tuple-element.476, f32[68,128,128]{2,1,0:T(8,128)} %fusion.70), kind=kCustom, calls=%fused_computation.5.clone.1 | custom fusion | flops 1114112 | bytes 13369616 | tf_op jit(solution)/shard_map/while/body/eval_jaxpr/scatter-add | solution.py:20
  628.6 10.6 %scatter_fusion = f32[128,28,128]{2,0,1:T(8,128)S(1)} fusion(f32[128,28,128]{2,0,1:T(8,128)S(1)} %get-tuple-element.503, s32[68]{0:T(128)S(1)} %get-tuple-element.473, f32[68,128,128]{2,1,0:T(8,128)} %fusion.69), kind=kCustom, calls=%fused_computation.4.clone.1 | custom fusion | flops 1114112 | bytes 13369616 | tf_op jit(solution)/shard_map/while/body/eval_jaxpr/scatter-add | solution.py:20
  651.0 315.3 %while.29 = (s32[]{:T(128)}, f32[128,32,128]{2,0,1:T(8,128)S(1)}, s32[8,68]{1,0:T(8,128)S(1)}, bf16[8,68,128,128]{3,2,1,0:T(8,128)(2,1)}, bf16[128,28,128]{2,0,1...) while((s32[]{:T(128)}, f32[128,32,128]{2,0,1:T(8,128)S(1)}, ...), condition=%wide.region_7.10_spmd, body=%wide.region_4.9_spmd.sunk | while | flops 574887424 | bytes 53490772 | solution.py:88
  659.8 10.6 %scatter_fusion.2 = f32[128,32,128]{2,0,1:T(8,128)S(1)} fusion(f32[128,32,128]{2,0,1:T(8,128)S(1)} %get-tuple-element.530, s32[68]{0:T(128)S(1)} %get-tuple-element.487, f32[68,128,128]{2,1,0:T(8,128)} %fusion.76), kind=kCustom, calls=%fused_computation.6.clone.1 | custom fusion | flops 1114112 | bytes 13369616 | tf_op jit(solution)/shard_map/while/body/eval_jaxpr/scatter-add | solution.py:27
  699.2 10.6 %scatter_fusion.2 = f32[128,32,128]{2,0,1:T(8,128)S(1)} fusion(f32[128,32,128]{2,0,1:T(8,128)S(1)} %get-tuple-element.530, s32[68]{0:T(128)S(1)} %get-tuple-element.487, f32[68,128,128]{2,1,0:T(8,128)} %fusion.76), kind=kCustom, calls=%fused_computation.6.clone.1 | custom fusion | flops 1114112 | bytes 13369616 | tf_op jit(solution)/shard_map/while/body/eval_jaxpr/scatter-add | solution.py:27
  738.6 10.6 %scatter_fusion.2 = f32[128,32,128]{2,0,1:T(8,128)S(1)} fusion(f32[128,32,128]{2,0,1:T(8,128)S(1)} %get-tuple-element.530, s32[68]{0:T(128)S(1)} %get-tuple-element.487, f32[68,128,128]{2,1,0:T(8,128)} %fusion.76), kind=kCustom, calls=%fused_computation.6.clone.1 | custom fusion | flops 1114112 | bytes 13369616 | tf_op jit(solution)/shard_map/while/body/eval_jaxpr/scatter-add | solution.py:27
  758.8 10.6 %scatter_fusion.3 = f32[128,32,128]{2,0,1:T(8,128)S(1)} fusion(f32[128,32,128]{2,0,1:T(8,128)S(1)} %scatter_fusion.2, s32[68]{0:T(128)S(1)} %get-tuple-element.490, f32[68,128,128]{2,1,0:T(8,128)} %fusion.77), kind=kCustom, calls=%fused_computation.7.clone.1 | custom fusion | flops 1114112 | bytes 13369616 | tf_op jit(solution)/shard_map/while/body/eval_jaxpr/scatter-add | solution.py:27
  778.0 10.6 %scatter_fusion.2 = f32[128,32,128]{2,0,1:T(8,128)S(1)} fusion(f32[128,32,128]{2,0,1:T(8,128)S(1)} %get-tuple-element.530, s32[68]{0:T(128)S(1)} %get-tuple-element.487, f32[68,128,128]{2,1,0:T(8,128)} %fusion.76), kind=kCustom, calls=%fused_computation.6.clone.1 | custom fusion | flops 1114112 | bytes 13369616 | tf_op jit(solution)/shard_map/while/body/eval_jaxpr/scatter-add | solution.py:27
  798.2 10.6 %scatter_fusion.3 = f32[128,32,128]{2,0,1:T(8,128)S(1)} fusion(f32[128,32,128]{2,0,1:T(8,128)S(1)} %scatter_fusion.2, s32[68]{0:T(128)S(1)} %get-tuple-element.490, f32[68,128,128]{2,1,0:T(8,128)} %fusion.77), kind=kCustom, calls=%fused_computation.7.clone.1 | custom fusion | flops 1114112 | bytes 13369616 | tf_op jit(solution)/shard_map/while/body/eval_jaxpr/scatter-add | solution.py:27
  817.4 10.6 %scatter_fusion.2 = f32[128,32,128]{2,0,1:T(8,128)S(1)} fusion(f32[128,32,128]{2,0,1:T(8,128)S(1)} %get-tuple-element.530, s32[68]{0:T(128)S(1)} %get-tuple-element.487, f32[68,128,128]{2,1,0:T(8,128)} %fusion.76), kind=kCustom, calls=%fused_computation.6.clone.1 | custom fusion | flops 1114112 | bytes 13369616 | tf_op jit(solution)/shard_map/while/body/eval_jaxpr/scatter-add | solution.py:27
  856.8 10.6 %scatter_fusion.2 = f32[128,32,128]{2,0,1:T(8,128)S(1)} fusion(f32[128,32,128]{2,0,1:T(8,128)S(1)} %get-tuple-element.530, s32[68]{0:T(128)S(1)} %get-tuple-element.487, f32[68,128,128]{2,1,0:T(8,128)} %fusion.76), kind=kCustom, calls=%fused_computation.6.clone.1 | custom fusion | flops 1114112 | bytes 13369616 | tf_op jit(solution)/shard_map/while/body/eval_jaxpr/scatter-add | solution.py:27
  877.0 10.6 %scatter_fusion.3 = f32[128,32,128]{2,0,1:T(8,128)S(1)} fusion(f32[128,32,128]{2,0,1:T(8,128)S(1)} %scatter_fusion.2, s32[68]{0:T(128)S(1)} %get-tuple-element.490, f32[68,128,128]{2,1,0:T(8,128)} %fusion.77), kind=kCustom, calls=%fused_computation.7.clone.1 | custom fusion | flops 1114112 | bytes 13369616 | tf_op jit(solution)/shard_map/while/body/eval_jaxpr/scatter-add | solution.py:27
  896.2 10.6 %scatter_fusion.2 = f32[128,32,128]{2,0,1:T(8,128)S(1)} fusion(f32[128,32,128]{2,0,1:T(8,128)S(1)} %get-tuple-element.530, s32[68]{0:T(128)S(1)} %get-tuple-element.487, f32[68,128,128]{2,1,0:T(8,128)} %fusion.76), kind=kCustom, calls=%fused_computation.6.clone.1 | custom fusion | flops 1114112 | bytes 13369616 | tf_op jit(solution)/shard_map/while/body/eval_jaxpr/scatter-add | solution.py:27
  916.4 10.6 %scatter_fusion.3 = f32[128,32,128]{2,0,1:T(8,128)S(1)} fusion(f32[128,32,128]{2,0,1:T(8,128)S(1)} %scatter_fusion.2, s32[68]{0:T(128)S(1)} %get-tuple-element.490, f32[68,128,128]{2,1,0:T(8,128)} %fusion.77), kind=kCustom, calls=%fused_computation.7.clone.1 | custom fusion | flops 1114112 | bytes 13369616 | tf_op jit(solution)/shard_map/while/body/eval_jaxpr/scatter-add | solution.py:27
  935.6 10.6 %scatter_fusion.2 = f32[128,32,128]{2,0,1:T(8,128)S(1)} fusion(f32[128,32,128]{2,0,1:T(8,128)S(1)} %get-tuple-element.530, s32[68]{0:T(128)S(1)} %get-tuple-element.487, f32[68,128,128]{2,1,0:T(8,128)} %fusion.76), kind=kCustom, calls=%fused_computation.6.clone.1 | custom fusion | flops 1114112 | bytes 13369616 | tf_op jit(solution)/shard_map/while/body/eval_jaxpr/scatter-add | solution.py:27
  969.3 68.6 %reduce-scatter.2.cloned.1.call-done = f32[32,4096]{1,0:T(8,128)} async-done(((f32[128,4096]{1,0:T(8,128)}), f32[32,4096]{1,0:T(8,128)}) %reduce-scatter.2.cloned.1.call-update) | async-done | bytes 524304 | tf_op jit(solution)/shard_map/reduce_scatter | solution.py:90
  (180 shorter events, 357.8 us)
Async XLA Ops:
  7.2 283.8 %all-gather.6.cloned.1.call-start = ((), (), s32[]{:S(2)}) async-start(), calls=%async_computation.2 | async-start | bytes 1310720 | tf_op jit(solution)/shard_map/all_gather | solution.py:32
  7.9 292.9 %all-gather.8.cloned.1.call-start = ((), (), s32[]{:S(2)}) async-start(), calls=%async_computation.4 | async-start | bytes 18382848 | tf_op jit(solution)/shard_map/all_gather | solution.py:42
  16.0 8.9 copy-start.7
  16.0 10.1 copy-start.5
  16.0 10.2 copy-start.6
  16.0 273.7 %copy-start.4 = (bf16[128,3584]{1,0:T(8,128)(2,1)S(1)}, bf16[128,3584]{1,0:T(8,128)(2,1)}, u32[]{:S(2)}) copy-start(bf16[128,3584]{1,0:T(8,128)(2,1)} %param.19) | copy-start | bytes 2752516
  16.0 284.8 %all-to-all-start = ((bf16[32,17,128,128]{3,2,1,0:T(8,128)(2,1)}), bf16[32,17,128,128]{3,2,1,0:T(8,128)(2,1)}, u32[]{:S(2)}, u32[]{:S(2)}) async-start(bf16[32,17,128,128]{3,2,1,0:T(8,128)(2,1)} %stack.3), calls=%async_computation | async-start | bytes 35651584 | tf_op jit(solution)/shard_map/all_to_all | solution.py:45
  24.8 1013.1 %reduce-scatter.2.cloned.1.call-start = ((), (), s32[]{:S(2)}) async-start(), calls=%async_computation.3 | async-start | bytes 2621440 | tf_op jit(solution)/shard_map/reduce_scatter | solution.py:90
  640.9 2.9 copy-start
  640.9 2.9 copy-start.1
  647.9 1.7 copy-start.3
  966.4 1.6 copy-start.2
Sparse Core Ops, SparseCore 0:
  9.7 26.4 all-gather.5
  38.4 261.8 all-gather.7
  968.1 69.7 reduce-scatter.1
